TPU v7x, 32 devices: a whole 2x2x4 slice. The times are simulated.
32 devices in a mesh: sample: 4 (over z), row: 2 (over y), col: 4 (over x, core).
Axes of the slice: x: 2, y: 2, z: 4, core: 2. Of those that a mesh axis runs over, the one named last changes fastest.
Arguments:
- single: bfloat16 [2048, 384], P(('sample', 'row')), parts along dimension 0, may hold values from -16 to 16
- pair_bias: bfloat16 [64, 512, 512], P('sample', 'row', 'col'), parts along dimension 0, may hold values from -4 to 400
- token_mask: int32 [2048], P('sample'), parts along dimension 0, may hold values from 0 to 1, as said below
- norm_gain: float32 [384], replicated, may hold values from 0.25 to 1.75
- w_query: bfloat16 [384, 384], replicated, may hold values from -0.3125 to 0.3125
- query_bias: float32 [384], replicated, may hold values from -3 to 3
- w_key: bfloat16 [384, 384], replicated, may hold values from -0.3125 to 0.3125
- w_value: bfloat16 [384, 384], replicated, may hold values from -0.3125 to 0.3125
- w_gate: bfloat16 [384, 384], replicated, may hold values from -0.3125 to 0.3125
- w_out: bfloat16 [384, 384], P(None, 'col'), may hold values from -0.3125 to 0.3125
Outputs:
- updated: float32 [2048, 384], P(('sample', 'row'), 'col'), parts along dimension 0
There are 4 independent parts, one for each index of `sample`. A program takes and returns all parts, laid end to end along the dimension named above; an argument that names none is the same for every part. Nothing has to cross between parts.
Inputs may be any that keep to these rules, and one draw needn't show every extreme that they name: `token_mask`: 1 for a leading run of 64 or more tokens and 0 for every token after it.
All inputs are finite; a program needn't handle non-finite values.
Results may differ from a plain program's by a relative error of at most 0.0014.
Values may be sent and summed in bfloat16 or wider, within the bound.
No kernel may reach another device: no remote copies, remote signals or barrier semaphores. Data moves between devices by JAX's collectives and lax.ppermute only.
A program may use at most 128 MiB of HBM per device.

v0:
```python
import math
import jax
import jax.numpy as jnp
from jax import lax
from jax.sharding import PartitionSpec as P

D = 384
HEADS = 16


def layer_norm(single, norm_gain):
    values_f32 = single.astype(jnp.float32)
    row_mean = jnp.mean(values_f32, axis=1, keepdims=True)
    centered = values_f32 - row_mean
    row_var = jnp.mean(centered * centered, axis=1, keepdims=True)
    return (centered * lax.rsqrt(row_var + 1e-05) * norm_gain).astype(jnp.bfloat16)


def attend(query_rows, key_rows, value_rows, bias_block, mask_cols):
    row_count = query_rows.shape[0]
    col_count = key_rows.shape[0]
    query_heads = query_rows.reshape(row_count, HEADS, -1)
    key_heads = key_rows.reshape(col_count, HEADS, -1)
    value_heads = value_rows.reshape(col_count, HEADS, -1)
    logits = jnp.einsum("qhd,khd->hqk", query_heads, key_heads, preferred_element_type=jnp.float32)
    mask_term = (mask_cols.astype(jnp.float32) - 1.0) * 1000000.0
    logits = logits + bias_block.astype(jnp.float32) + mask_term[None, None, :]
    row_peak = jnp.max(logits, axis=2)
    exp_scores = jnp.exp(logits - row_peak[:, :, None])
    row_total = jnp.sum(exp_scores, axis=2)
    weighted = jnp.einsum(
        "hqk,khd->qhd",
        exp_scores.astype(jnp.bfloat16),
        value_heads,
        preferred_element_type=jnp.float32,
    )
    return (row_peak.T, row_total.T, weighted.reshape(row_count, -1))


def on_device(
    single, pair_bias, token_mask, norm_gain, w_query, query_bias, w_key, w_value, w_gate, w_out
):
    head_dim = D // HEADS
    inv_sqrt = 1.0 / math.sqrt(head_dim)
    tok_rows = single.shape[0]
    col_total = lax.axis_size("col")
    out_width = w_out.shape[1]
    col_pos = lax.axis_index("col")
    normed = layer_norm(single, norm_gain)
    query = (
        (jnp.dot(normed, w_query, preferred_element_type=jnp.float32) + query_bias) * inv_sqrt
    ).astype(jnp.bfloat16)
    gate_act = jax.nn.sigmoid(jnp.dot(normed, w_gate, preferred_element_type=jnp.float32))
    single_cols = lax.dynamic_slice_in_dim(single, col_pos * out_width, out_width, 1).astype(
        jnp.float32
    )
    key_local = jnp.dot(normed, w_key, preferred_element_type=jnp.float32).astype(jnp.bfloat16)
    value_local = jnp.dot(normed, w_value, preferred_element_type=jnp.float32).astype(jnp.bfloat16)
    key_all, value_all = (
        lax.all_gather(key_local, "row", axis=0, tiled=True),
        lax.all_gather(value_local, "row", axis=0, tiled=True),
    )
    sub_rows = tok_rows // col_total
    query_start = col_pos * sub_rows
    bias_panel = lax.all_to_all(pair_bias, "col", split_axis=1, concat_axis=2, tiled=True)
    key_rows, value_rows = (key_all, value_all)
    query_part = lax.dynamic_slice_in_dim(query, query_start, sub_rows, 0)
    gate_part = lax.dynamic_slice_in_dim(gate_act, query_start, sub_rows, 0)
    row_peak, row_total, weighted = attend(query_part, key_rows, value_rows, bias_panel, token_mask)
    attended = weighted / jnp.repeat(row_total, head_dim, axis=1)
    gated_part = (gate_part * attended).astype(jnp.bfloat16)
    gated_all = lax.all_gather(gated_part, "col", axis=0, tiled=True)
    result = single_cols + jnp.dot(gated_all, w_out, preferred_element_type=jnp.float32)
    return result


def solution(mesh):
    return jax.shard_map(
        on_device,
        mesh=mesh,
        in_specs=(
            P(("sample", "row"), None),
            P("sample", "row", "col"),
            P("sample"),
            P(),
            P(),
            P(),
            P(),
            P(),
            P(),
            P(None, "col"),
        ),
        out_specs=P(("sample", "row"), "col"),
        check_vma=False,
    )
```

profile of v0, /device:TPU:0, one launch (start us, length us, event | category | flops | bytes accessed | tf_op | source)
XLA Modules:
  0.0 40.1 jit_solution(15966717443112249602)
XLA Ops:
  0.0 0.0 copy-start
  0.0 2.9 %copy.31 = bf16[16,256,128]{2,0,1:T(8,128)(2,1)} copy(bf16[16,256,128]{2,1,0:T(8,128)(2,1)} %param.11) | data formatting | bytes 2097152 | tf_op args[1]
  3.0 4.4 %all-to-all-start = ((bf16[16,256,128]{2,0,1:T(8,128)(2,1)}), bf16[16,256,128]{2,0,1:T(8,128)(2,1)S(1)}, u32[]{:S(2)}, u32[]{:S(2)}) async-start(bf16[16,256,128]{2,0,1:T(8,128)(2,1)} %copy.31), calls=%async_computation | async-start | bytes 2097152 | tf_op jit(solution)/shard_map/all_to_all | solution.py:65
  7.3 0.0 copy-done.1
  7.3 0.1 convert_reduce_fusion
  7.5 0.2 fusion.7
  7.7 0.0 copy-done
  7.7 0.3 convolution_convert_fusion.1
  8.0 0.0 copy-done.2
  8.0 0.3 fusion.18
  8.4 0.0 copy-start.7
  8.4 0.0 copy-start.3
  8.4 0.3 convolution_convert_fusion
  8.8 8.5 %all_gather.9 = bf16[512,384]{1,0:T(8,128)(2,1)S(1)} all-gather(bf16[256,384]{1,0:T(8,128)(2,1)S(1)} %convolution_convert_fusion.1), channel_id=1, replica_groups=mesh['sample'=4,'row'=2,'col'=4] {'row'}, dimensions={0}, use_global_device_ids=true | all-gather | bytes 589824 | tf_op jit(solution)/shard_map/all_gather | solution.py:61
  17.3 0.2 copy.28
  17.5 0.1 copy.29
  17.6 7.3 %all_gather.10 = bf16[512,384]{1,0:T(8,128)(2,1)S(1)} all-gather(bf16[256,384]{1,0:T(8,128)(2,1)S(1)} %convolution_convert_fusion), channel_id=1, replica_groups=mesh['sample'=4,'row'=2,'col'=4] {'row'}, dimensions={0}, use_global_device_ids=true | all-gather | bytes 589824 | tf_op jit(solution)/shard_map/all_gather | solution.py:60
  24.9 0.2 copy.30
  25.1 0.1 constant_dynamic-slice_fusion
  25.3 0.1 copy.34
  25.4 1.1 %fusion.21 = f32[256,384]{1,0:T(8,128)} fusion(bf16[384,384]{1,0:T(8,128)(2,1)S(1)} %copy-done.3, bf16[256,384]{1,0:T(8,128)(2,1)S(1)} %copy-done.1, f32[384]{0:T(512)S(1)} %copy-done.5, f32[256]{0:T(256)S(1)} %add_rsqrt_fusion, f32[256]{0:T(256)S(1)} %broadcast_multiply_fusion), kind=kOutput, calls=%fused_computation.32 | convolution fusion | flops 75988992 | bytes 888320 | tf_op jit(solution)/shard_map/dot_general | solution.py:53
  26.5 0.0 all-to-all-done
  26.5 2.2 %copy.36 = f32[16,4,64,128]{3,1,2,0:T(4,128)} copy(bf16[16,4,64,128]{3,0,2,1:T(8,128)(2,1)S(1)} %bitcast.24) | data formatting | bytes 3145728 | tf_op jit(solution)/shard_map/convert_element_type | solution.py:27
  28.6 2.1 %reshape.37 = f32[16,64,512]{2,1,0:T(8,128)S(1)} reshape(f32[16,64,4,128]{3,2,1,0:T(4,128)} %bitcast.23) | data formatting | bytes 4194304 | tf_op jit(solution)/shard_map/convert_element_type | solution.py:27
  30.7 0.6 %fusion.23 = (f32[16,64]{1,0:T(8,128)S(1)}, f32[16,64,512]{2,1,0:T(8,128)S(1)}) fusion(f32[512]{0:T(512)S(1)} %add_multiply_fusion, f32[16,64,512]{2,1,0:T(8,128)S(1)} %reshape.37, bf16[64,16,24]{0,2,1:T(8,128)(2,1)S(1)} %bitcast.28, bf16[512,16,24]{0,2,1:T(8,128)(2,1)S(1)} %bitcast.25), kind=kOutput, calls=%fused_computation.33 | convolution fusion | flops 26737664 | bytes 4642816 | tf_op jit(solution)/shard_map/qhd,khd->hqk/dot_general | solution.py:25
  31.3 0.8 %fusion = f32[16,64]{1,0:T(8,128)S(1)} fusion(f32[16,64,512]{2,1,0:T(8,128)S(1)} %get-tuple-element.6, f32[16,64]{1,0:T(8,128)S(1)} %get-tuple-element.5), kind=kLoop, calls=%fused_computation.3 | loop fusion | flops 1047552 | bytes 2105344 | tf_op jit(solution)/shard_map/reduce_sum | solution.py:30
  32.1 0.0 copy-start.4
  32.1 0.5 %fusion.2 = f32[64,16,24]{0,2,1:T(8,128)S(1)} fusion(bf16[512,16,24]{0,2,1:T(8,128)(2,1)S(1)} %bitcast.26, f32[16,64,512]{2,1,0:T(8,128)S(1)} %get-tuple-element.6, f32[16,64]{1,0:T(8,128)S(1)} %get-tuple-element.5, f32[64,16]{0,1:T(8,128)S(1)} %bitcast.29), kind=kOutput, calls=%fused_computation.8 | convolution fusion | flops 26238976 | bytes 2596864 | tf_op jit(solution)/shard_map/hqk,khd->qhd/dot_general | solution.py:31
  32.6 0.1 copy.33
  32.7 0.9 %fusion.16 = bf16[64,384]{1,0:T(8,128)(2,1)S(1)} fusion(f32[64,384]{1,0:T(8,128)S(1)} %copy.33, f32[256,384]{1,0:T(8,128)} %fusion.21, s32[]{:T(128)S(6)} %select_n.8), kind=kLoop, calls=%fused_computation.26 | loop fusion | flops 122880 | bytes 245764 | tf_op jit(solution)/shard_map/convert_element_type | solution.py:71
  33.7 5.6 %all_gather.11 = bf16[256,384]{1,0:T(8,128)(2,1)S(1)} all-gather(bf16[64,384]{1,0:T(8,128)(2,1)S(1)} %fusion.16), channel_id=1, replica_groups=mesh['sample'=4,'row'=2,'col'=4] {'col'}, dimensions={0}, use_global_device_ids=true | all-gather | bytes 245760 | tf_op jit(solution)/shard_map/all_gather | solution.py:72
  39.3 0.8 %convolution_add_fusion = f32[256,96]{0,1:T(8,128)} fusion(bf16[256,384]{1,0:T(8,128)(2,1)S(1)} %all_gather.11, bf16[384,96]{0,1:T(8,128)(2,1)S(1)} %copy-done.4, bf16[256,96]{0,1:T(8,128)(2,1)S(1)} %copy.34), kind=kOutput, calls=%fused_computation.9 | convolution fusion | flops 18923520 | bytes 417792 | tf_op jit(solution)/shard_map/dot_general | solution.py:73
  (15 shorter events, 0.1 us)
Async XLA Ops:
  0.0 7.7 %copy-start = (bf16[384,384]{1,0:T(8,128)(2,1)S(1)}, bf16[384,384]{1,0:T(8,128)(2,1)}, u32[]{:S(2)}) copy-start(bf16[384,384]{1,0:T(8,128)(2,1)} %param.17) | copy-start | bytes 884740
  0.0 7.3 %copy-start.1 = (bf16[256,384]{1,0:T(8,128)(2,1)S(1)}, bf16[256,384]{1,0:T(8,128)(2,1)}, u32[]{:S(2)}) copy-start(bf16[256,384]{1,0:T(8,128)(2,1)} %param.10) | copy-start | bytes 589828
  0.0 7.7 %copy-start.5 = (f32[384]{0:T(512)S(1)}, f32[384]{0:T(512)}, u32[]{:S(2)}) copy-start(f32[384]{0:T(512)} %param.13) | copy-start | bytes 4612
  3.0 5.1 %copy-start.2 = (bf16[384,384]{1,0:T(8,128)(2,1)S(1)}, bf16[384,384]{1,0:T(8,128)(2,1)}, u32[]{:S(2)}) copy-start(bf16[384,384]{1,0:T(8,128)(2,1)} %param.14) | copy-start | bytes 884740
  3.0 5.5 %copy-start.8 = (bf16[384,384]{1,0:T(8,128)(2,1)S(1)}, bf16[384,384]{1,0:T(8,128)(2,1)}, u32[]{:S(2)}) copy-start(bf16[384,384]{1,0:T(8,128)(2,1)} %param.16) | copy-start | bytes 884740
  3.0 5.8 %copy-start.6 = (f32[384]{0:T(512)S(1)}, f32[384]{0:T(512)}, u32[]{:S(2)}) copy-start(f32[384]{0:T(512)} %param.15) | copy-start | bytes 4612
  3.0 23.5 %all-to-all-start = ((bf16[16,256,128]{2,0,1:T(8,128)(2,1)}), bf16[16,256,128]{2,0,1:T(8,128)(2,1)S(1)}, u32[]{:S(2)}, u32[]{:S(2)}) async-start(bf16[16,256,128]{2,0,1:T(8,128)(2,1)} %copy.31), calls=%async_computation | async-start | bytes 2097152 | tf_op jit(solution)/shard_map/all_to_all | solution.py:65
  8.4 17.0 %copy-start.7 = (s32[512]{0:T(512)S(1)}, s32[512]{0:T(512)}, u32[]{:S(2)}) copy-start(s32[512]{0:T(512)} %param.12) | copy-start | bytes 6148
  8.4 17.0 %copy-start.3 = (bf16[384,384]{1,0:T(8,128)(2,1)S(1)}, bf16[384,384]{1,0:T(8,128)(2,1)}, u32[]{:S(2)}) copy-start(bf16[384,384]{1,0:T(8,128)(2,1)} %param.18) | copy-start | bytes 884740
  32.1 7.2 %copy-start.4 = (bf16[384,96]{0,1:T(8,128)(2,1)S(1)}, bf16[384,96]{0,1:T(8,128)(2,1)}, u32[]{:S(2)}) copy-start(bf16[384,96]{0,1:T(8,128)(2,1)} %param.19) | copy-start | bytes 221188
where the time goes:
time: 40.4 us; the launch traced here: 40.1 us
  blocking collectives  21.4 us (53%)
  local copies, waits for them, and re-layouts  8.06 us (20%)
  starting transfers between devices  4.38 us (11%)
  matrix products  4.02 us (10%)
  other arithmetic  2.06 us (5%)
    all_gather x1, blocking collectives, on_device(): lax.all_gather(value_local, 'row', axis=0, tiled=True)  8.47 us
    all_gather x1, blocking collectives, on_device(): lax.all_gather(key_local, 'row', axis=0, tiled=True)  7.34 us
    all_gather x1, blocking collectives, on_device(): gated_all = lax.all_gather(gated_part, 'col', axis=0, tiled=True)  5.6 us
    all_to_all x1, starting transfers between devices, on_device(): lax.all_to_all(pair_bias, 'col', split_axis=1, concat_axis=2, tiled=True)  4.38 us
    convert_element_type x2, local copies, waits for them, and re-layouts, attend(): logits = logits + bias_block.astype(jnp.float32) + mask_term[None, None, :]  4.25 us
    unnamed x20, local copies, waits for them, and re-layouts  3.08 us
    dot_general x1, matrix products, on_device(): jnp.dot(normed, w_gate, preferred_element_type=jnp.float32)  1.09 us
    convert_element_type x1, other arithmetic, on_device(): gated_part = (gate_part * attended).astype(jnp.bfloat16)  0.94 us
  transfers between devices with their start and end apart: 1, of which 0 were waited for; matrix products, arithmetic and copies ran while one was open for 8% of the time, Pallas kernels for 0%

commit v1 on v0

--- a/solution.py
+++ b/solution.py
@@ -62,7 +62,10 @@
     )
     sub_rows = tok_rows // col_total
     query_start = col_pos * sub_rows
-    bias_panel = lax.all_to_all(pair_bias, "col", split_axis=1, concat_axis=2, tiled=True)
+    bias_panel = jnp.concatenate(
+        lax.all_to_all(jnp.stack(jnp.split(pair_bias, lax.axis_size("col"), axis=1)), "col", 0, 0),
+        axis=2,
+    )
     key_rows, value_rows = (key_all, value_all)
     query_part = lax.dynamic_slice_in_dim(query, query_start, sub_rows, 0)
     gate_part = lax.dynamic_slice_in_dim(gate_act, query_start, sub_rows, 0)

time: 40.4 us -> 34 us (0.84)
  local copies, waits for them, and re-layouts: 8.06 us -> 2.17 us
  matrix products: 4.02 us -> 3.26 us
    convert_element_type x2 -> x0, local copies, waits for them, and re-layouts: 4.25 us -> none  [attend(): logits = logits + bias_block.astype(jnp.float32) + mask_term[None, None, :]]
    unnamed x20 -> x19, local copies, waits for them, and re-layouts: 3.08 us -> 0.15 us
    another operation x0 -> x1, local copies, waits for them, and re-layouts: none -> 1.31 us  [on_device(): jnp.stack(jnp.split(pair_bias, lax.axis_size('col'), axis=1))]
    all_gather x1, blocking collectives: 7.34 us -> 8.48 us  [on_device(): lax.all_gather(key_local, 'row', axis=0, tiled=True)]
    all_gather x1, blocking collectives: 8.47 us -> 7.35 us  [on_device(): lax.all_gather(value_local, 'row', axis=0, tiled=True)]
    another operation x0 -> x1, other arithmetic: none -> 1.11 us  [on_device(): jnp.stack(jnp.split(pair_bias, lax.axis_size('col'), axis=1))]
    convert_element_type x1, other arithmetic: 0.94 us -> 0.04 us  [on_device(): gated_part = (gate_part * attended).astype(jnp.bfloat16)]
    dot_general x1, matrix products: 1.09 us -> 0.33 us  [on_device(): jnp.dot(normed, w_gate, preferred_element_type=jnp.float32)]
  transfers between devices with their start and end apart: 1 -> 1, of which waited for: 0 -> 0; matrix products, arithmetic and copies ran while one was open for 8% -> 7% of each run, Pallas kernels for 0% -> 0%
where the time goes in v1:
time: 34 us; the launch traced here: 33.7 us
  blocking collectives  21.4 us (63%)
  starting transfers between devices  4.37 us (13%)
  matrix products  3.26 us (10%)
  other arithmetic  2.27 us (7%)
  local copies, waits for them, and re-layouts  2.17 us (6%)
    all_gather x1, blocking collectives, on_device(): lax.all_gather(key_local, 'row', axis=0, tiled=True)  8.48 us
    all_gather x1, blocking collectives, on_device(): lax.all_gather(value_local, 'row', axis=0, tiled=True)  7.35 us
    all_gather x1, blocking collectives, on_device(): gated_all = lax.all_gather(gated_part, 'col', axis=0, tiled=True)  5.6 us
    all_to_all x1, starting transfers between devices, on_device(): lax.all_to_all(jnp.stack(jnp.split(pair_bias, lax.axis_size('col'), axis=...  4.37 us
    another operation x1, local copies, waits for them, and re-layouts, on_device(): jnp.stack(jnp.split(pair_bias, lax.axis_size('col'), axis=1))  1.31 us
    another operation x1, other arithmetic, on_device(): jnp.stack(jnp.split(pair_bias, lax.axis_size('col'), axis=1))  1.11 us
    dot_general x1, matrix products, on_device(): jnp.dot(gated_all, w_out, preferred_element_type=jnp.float32)  0.85 us
    reduce_sum x1, other arithmetic, attend(): row_total = jnp.sum(exp_scores, axis=2)  0.78 us
  transfers between devices with their start and end apart: 1, of which 0 were waited for; matrix products, arithmetic and copies ran while one was open for 7% of the time, Pallas kernels for 0%

profile of v1, /device:TPU:0, one launch (start us, length us, event | category | flops | bytes accessed | tf_op | source)
XLA Modules:
  0.0 33.7 jit_solution(9422909382869816491)
XLA Ops:
  0.0 0.0 copy-start
  0.0 1.3 %slice_bitcast_fusion.3 = (bf16[1,16,64,128]{3,2,1,0:T(8,128)(2,1)S(1)}, bf16[1,16,64,128]{3,2,1,0:T(8,128)(2,1)S(1)}, bf16[1,16,64,128]{3,2,1,0:T(8,128)(2,1)S(1)}, bf16[1,16,64,128]{3,2,1,0:T(8,128)(2,1)S(1)}) fusion(bf16[16,256,128]{2,1,0:T(8,128)(2,1)} %param.11), kind=kLoop, calls=%fused_computation.23 | loop fusion | bytes 2097152 | tf_op jit(solution)/shard_map/stack | solution.py:66
  1.3 0.0 copy-start.1
  1.3 0.0 copy-start.4
  1.3 1.1 %pad_maximum_fusion = bf16[4,16,64,128]{3,2,1,0:T(8,128)(2,1)} fusion(bf16[1,16,64,128]{3,2,1,0:T(8,128)(2,1)S(1)} %get-tuple-element.7, bf16[1,16,64,128]{3,2,1,0:T(8,128)(2,1)S(1)} %get-tuple-element.8, bf16[1,16,64,128]{3,2,1,0:T(8,128)(2,1)S(1)} %get-tuple-element.6, bf16[1,16,64,128]{3,2,1,0:T(8,128)(2,1)S(1)} %get-tuple-element.5), kind=kLoop, calls=%fused_computation.11 | loop fusion | flops 1572864 | bytes 2097152 | tf_op jit(solution)/shard_map/stack | solution.py:66
  2.5 4.4 %all-to-all-start = ((bf16[4,16,64,128]{3,2,1,0:T(8,128)(2,1)}), bf16[4,16,64,128]{3,2,1,0:T(8,128)(2,1)S(1)}, u32[]{:S(2)}, u32[]{:S(2)}) async-start(bf16[4,16,64,128]{3,2,1,0:T(8,128)(2,1)} %pad_maximum_fusion), calls=%async_computation | async-start | bytes 2097152 | tf_op jit(solution)/shard_map/all_to_all | solution.py:66
  6.8 0.0 copy-done.1
  6.8 0.1 convert_reduce_fusion
  7.0 0.2 fusion.8
  7.2 0.0 copy-done
  7.2 0.3 fusion.19
  7.5 0.3 convolution_convert_fusion
  7.9 0.0 copy-start.6
  7.9 0.0 copy-start.2
  7.9 0.3 convolution_convert_fusion.1
  8.3 0.1 copy.28
  8.4 8.5 %all_gather.10 = bf16[512,384]{1,0:T(8,128)(2,1)S(1)} all-gather(bf16[256,384]{1,0:T(8,128)(2,1)S(1)} %convolution_convert_fusion), channel_id=1, replica_groups=mesh['sample'=4,'row'=2,'col'=4] {'row'}, dimensions={0}, use_global_device_ids=true | all-gather | bytes 589824 | tf_op jit(solution)/shard_map/all_gather | solution.py:60
  16.9 0.2 copy.29
  17.1 7.4 %all_gather.9 = bf16[512,384]{1,0:T(8,128)(2,1)S(1)} all-gather(bf16[256,384]{1,0:T(8,128)(2,1)S(1)} %convolution_convert_fusion.1), channel_id=1, replica_groups=mesh['sample'=4,'row'=2,'col'=4] {'row'}, dimensions={0}, use_global_device_ids=true | all-gather | bytes 589824 | tf_op jit(solution)/shard_map/all_gather | solution.py:61
  24.4 0.2 copy.27
  24.6 0.1 constant_dynamic-slice_fusion
  24.7 0.1 copy.32
  24.9 0.3 fusion.22
  25.2 0.0 all-to-all-done
  25.2 0.6 %fusion.24 = (f32[16,64]{1,0:T(8,128)S(1)}, f32[16,64,512]{2,1,0:T(8,128)S(1)}) fusion(f32[512]{0:T(512)S(1)} %add_multiply_fusion, bf16[64,16,24]{0,2,1:T(8,128)(2,1)S(1)} %bitcast.37, bf16[512,16,24]{0,2,1:T(8,128)(2,1)S(1)} %bitcast.34, bf16[4,16,64,128]{3,2,1,0:T(8,128)(2,1)S(1)} %all-to-all-done), kind=kOutput, calls=%fused_computation.39 | convolution fusion | flops 27261952 | bytes 3594240 | tf_op jit(solution)/shard_map/qhd,khd->hqk/dot_general | solution.py:25
  25.8 0.8 %fusion.1 = f32[16,64]{1,0:T(8,128)S(1)} fusion(f32[16,64,512]{2,1,0:T(8,128)S(1)} %get-tuple-element.10, f32[16,64]{1,0:T(8,128)S(1)} %get-tuple-element.9), kind=kLoop, calls=%fused_computation.4 | loop fusion | flops 1047552 | bytes 2105344 | tf_op jit(solution)/shard_map/reduce_sum | solution.py:30
  26.6 0.0 copy-start.3
  26.6 0.5 %fusion.3 = f32[64,16,24]{0,2,1:T(8,128)S(1)} fusion(bf16[512,16,24]{0,2,1:T(8,128)(2,1)S(1)} %bitcast.35, f32[16,64,512]{2,1,0:T(8,128)S(1)} %get-tuple-element.10, f32[16,64]{1,0:T(8,128)S(1)} %get-tuple-element.9, f32[64,16]{0,1:T(8,128)S(1)} %bitcast.38), kind=kOutput, calls=%fused_computation.9 | convolution fusion | flops 26238976 | bytes 2596864 | tf_op jit(solution)/shard_map/hqk,khd->qhd/dot_general | solution.py:31
  27.1 0.1 copy.31
  27.3 5.6 %all_gather.11 = bf16[256,384]{1,0:T(8,128)(2,1)S(1)} all-gather(bf16[64,384]{1,0:T(8,128)(2,1)S(1)} %fusion.17), channel_id=1, replica_groups=mesh['sample'=4,'row'=2,'col'=4] {'col'}, dimensions={0}, use_global_device_ids=true | all-gather | bytes 245760 | tf_op jit(solution)/shard_map/all_gather | solution.py:75
  32.9 0.0 copy-done.3
  32.9 0.9 %convolution_add_fusion = f32[256,96]{0,1:T(8,128)} fusion(bf16[256,384]{1,0:T(8,128)(2,1)S(1)} %all_gather.11, bf16[384,96]{0,1:T(8,128)(2,1)S(1)} %copy-done.3, bf16[256,96]{0,1:T(8,128)(2,1)S(1)} %copy.32), kind=kOutput, calls=%fused_computation.10 | convolution fusion | flops 18923520 | bytes 417792 | tf_op jit(solution)/shard_map/dot_general | solution.py:76
  (14 shorter events, 0.1 us)
Async XLA Ops:
  0.0 7.2 %copy-start = (bf16[384,384]{1,0:T(8,128)(2,1)S(1)}, bf16[384,384]{1,0:T(8,128)(2,1)}, u32[]{:S(2)}) copy-start(bf16[384,384]{1,0:T(8,128)(2,1)} %param.14) | copy-start | bytes 884740
  1.3 5.5 %copy-start.1 = (bf16[256,384]{1,0:T(8,128)(2,1)S(1)}, bf16[256,384]{1,0:T(8,128)(2,1)}, u32[]{:S(2)}) copy-start(bf16[256,384]{1,0:T(8,128)(2,1)} %param.10) | copy-start | bytes 589828
  1.3 5.9 %copy-start.4 = (f32[384]{0:T(512)S(1)}, f32[384]{0:T(512)}, u32[]{:S(2)}) copy-start(f32[384]{0:T(512)} %param.13) | copy-start | bytes 4612
  2.4 5.1 %copy-start.7 = (bf16[384,384]{1,0:T(8,128)(2,1)S(1)}, bf16[384,384]{1,0:T(8,128)(2,1)}, u32[]{:S(2)}) copy-start(bf16[384,384]{1,0:T(8,128)(2,1)} %param.16) | copy-start | bytes 884740
  2.4 5.4 %copy-start.8 = (bf16[384,384]{1,0:T(8,128)(2,1)S(1)}, bf16[384,384]{1,0:T(8,128)(2,1)}, u32[]{:S(2)}) copy-start(bf16[384,384]{1,0:T(8,128)(2,1)} %param.17) | copy-start | bytes 884740
  2.5 5.8 %copy-start.5 = (f32[384]{0:T(512)S(1)}, f32[384]{0:T(512)}, u32[]{:S(2)}) copy-start(f32[384]{0:T(512)} %param.15) | copy-start | bytes 4612
  2.5 22.8 %all-to-all-start = ((bf16[4,16,64,128]{3,2,1,0:T(8,128)(2,1)}), bf16[4,16,64,128]{3,2,1,0:T(8,128)(2,1)S(1)}, u32[]{:S(2)}, u32[]{:S(2)}) async-start(bf16[4,16,64,128]{3,2,1,0:T(8,128)(2,1)} %pad_maximum_fusion), calls=%async_computation | async-start | bytes 2097152 | tf_op jit(solution)/shard_map/all_to_all | solution.py:66
  7.9 17.0 %copy-start.6 = (s32[512]{0:T(512)S(1)}, s32[512]{0:T(512)}, u32[]{:S(2)}) copy-start(s32[512]{0:T(512)} %param.12) | copy-start | bytes 6148
  7.9 17.0 %copy-start.2 = (bf16[384,384]{1,0:T(8,128)(2,1)S(1)}, bf16[384,384]{1,0:T(8,128)(2,1)}, u32[]{:S(2)}) copy-start(bf16[384,384]{1,0:T(8,128)(2,1)} %param.18) | copy-start | bytes 884740
  26.6 6.3 %copy-start.3 = (bf16[384,96]{0,1:T(8,128)(2,1)S(1)}, bf16[384,96]{0,1:T(8,128)(2,1)}, u32[]{:S(2)}) copy-start(bf16[384,96]{0,1:T(8,128)(2,1)} %param.19) | copy-start | bytes 221188
